TPU v7x, 512 devices: a whole 4x4x16 slice. The times are simulated.
512 devices in a mesh: row: 16 (over z), col: 32 (over y, x, core).
Axes of the slice: x: 4, y: 4, z: 16, core: 2. Of those that a mesh axis runs over, the one named last changes fastest.
Arguments:
- right_side: bfloat16 [16384, 16384], P('row', 'col'), may hold values from -180 to 180
- theta_left: bfloat16 [512, 16384], P(None, 'row'), may hold values from -0.125 to 0.125
- theta_right: bfloat16 [512, 16384], P(None, 'col'), may hold values from -0.125 to 0.125
- query_rows: int32 [1024, 2], replicated, may hold values from 0 to 16384, as said below
- query_cols: int32 [1024, 2], replicated, may hold values from 0 to 16384, as said below
Outputs:
- residual: float32 [16384, 16384], P('row', 'col')
- step_ratio: float32 [1], replicated
- answers: float32 [1024], replicated
Inputs may be any that keep to these rules, and one draw needn't show every extreme that they name: `query_rows`: each row is a start and an end with 0 <= start < end <= 16384. `query_cols`: each row is a start and an end with 0 <= start < end <= 16384.
All inputs are finite; a program needn't handle non-finite values.
Results may differ from a plain program's by a relative error of at most 0.0003.
Values sent between devices are 32-bit elements; how exact they have to be, the bound alone decides.
A program may use at most 64 MiB of HBM per device.

v0:
```python
import jax
import jax.numpy as jnp
from jax import lax
from jax.sharding import PartitionSpec as P


def prefix_2(part, axis, combine, identity):
    place = lax.axis_index(axis)
    gathered = lax.all_gather(part, axis)
    state = jnp.zeros_like(part) + jnp.asarray(identity, part.dtype)

    def one(hop, state):
        return combine(state, lax.dynamic_index_in_dim(gathered, hop, 0, False))

    return lax.fori_loop(0, place, one, state)


def add_pair(earlier, later):
    return earlier + later


def cum_last(values):
    length = values.shape[1]
    block_len = 128
    index_line = jnp.arange(block_len)
    upper_tri = (index_line[:, None] <= index_line[None, :]).astype(jnp.float32)
    pieces = values.reshape(values.shape[0], length // block_len, block_len)
    within = jnp.einsum("rbk,kj->rbj", pieces, upper_tri, precision=lax.Precision.HIGHEST)
    totals = within[:, :, -1]
    carried = jnp.cumsum(totals, axis=1) - totals
    return (within + carried[:, :, None]).reshape(values.shape)


def cum_first(values):
    length = values.shape[0]
    block_len = 128
    index_line = jnp.arange(block_len)
    lower_tri = (index_line[:, None] >= index_line[None, :]).astype(jnp.float32)
    pieces = values.reshape(length // block_len, block_len, values.shape[1])
    within = jnp.einsum("ik,bkc->bic", lower_tri, pieces, precision=lax.Precision.HIGHEST)
    totals = within[:, -1, :]
    carried = jnp.cumsum(totals, axis=0) - totals
    return (within + carried[:, None, :]).reshape(values.shape)


def down_scan(column_totals):
    return prefix_2(column_totals, "row", add_pair, jnp.zeros_like(column_totals))


def shards(right_side, theta_left, theta_right, query_rows, query_cols):
    highest = lax.Precision.HIGHEST
    block_rows, block_cols = right_side.shape
    start_field = right_side.astype(jnp.float32)
    left_wide = theta_left.astype(jnp.float32)
    right_wide = theta_right.astype(jnp.float32)
    start_norm = lax.psum(jnp.sum(start_field * start_field), ("row", "col"))
    partial_right = lax.dot_general(
        right_side, theta_right, (((1,), (1,)), ((), ())), preferred_element_type=jnp.float32
    )
    summed_right = lax.psum(partial_right, "col")
    middle = start_field + jnp.dot(
        summed_right, right_wide, precision=highest, preferred_element_type=jnp.float32
    )
    partial_left = jnp.dot(left_wide, middle, precision=highest, preferred_element_type=jnp.float32)
    summed_left = lax.psum(partial_left, "row")
    image_field = middle + lax.dot_general(
        left_wide,
        summed_left,
        (((0,), (0,)), ((), ())),
        precision=highest,
        preferred_element_type=jnp.float32,
    )
    curvature = lax.psum(jnp.sum(start_field * image_field), ("row", "col"))
    alpha_step = start_norm / curvature
    residual = start_field - alpha_step * image_field
    fresh = lax.psum(jnp.sum(residual * residual), ("row", "col"))
    step_ratio = (fresh / start_norm).reshape(1)
    solution = alpha_step * start_field
    across = cum_last(solution)
    row_totals = across[:, -1]
    left_carry = prefix_2(row_totals, "col", add_pair, jnp.zeros_like(row_totals))
    vertical = cum_first(across + left_carry[:, None])
    upper_carry = down_scan(vertical[-1, :])
    prefix = vertical + upper_carry[None, :]
    row_start = lax.axis_index("row") * block_rows
    col_start = lax.axis_index("col") * block_cols
    flat_prefix = prefix.reshape(-1)

    def corner_value(row_bound, col_bound):
        local_row = row_bound - 1 - row_start
        local_col = col_bound - 1 - col_start
        inside = (
            (local_row >= 0)
            & (local_row < block_rows)
            & (local_col >= 0)
            & (local_col < block_cols)
        )
        position_flat = jnp.clip(local_row, 0, block_rows - 1) * block_cols + jnp.clip(
            local_col, 0, block_cols - 1
        )
        return jnp.where(inside, jnp.take(flat_prefix, position_flat), 0.0)

    low_row = query_rows[:, 0]
    high_row = query_rows[:, 1]
    low_col = query_cols[:, 0]
    high_col = query_cols[:, 1]
    partial_answers = (
        corner_value(high_row, high_col)
        - corner_value(low_row, high_col)
        - corner_value(high_row, low_col)
        + corner_value(low_row, low_col)
    )
    combined = lax.psum(partial_answers, ("row", "col"))
    area = (high_row - low_row).astype(jnp.float32) * (high_col - low_col).astype(jnp.float32)
    answers = combined / jnp.sqrt(area)
    return (residual, step_ratio, answers)


def solution(mesh):
    return jax.shard_map(
        shards,
        mesh=mesh,
        in_specs=(P("row", "col"), P(None, "row"), P(None, "col"), P(), P()),
        out_specs=(P("row", "col"), P(), P()),
        check_vma=False,
    )
```

profile of v0, /device:TPU:1, one launch (start us, length us, event | category | flops | bytes accessed | tf_op | source)
XLA Modules:
  0.0 611.5 jit_solution(15123079067743380518)
XLA Ops:
  7.2 3.5 fusion.25
  10.9 144.4 %all-reduce.5.cloned.1.call-done = f32[1024,512]{1,0:T(8,128)} async-done(((f32[1024,512]{1,0:T(8,128)}), f32[1024,512]{1,0:T(8,128)}) %all-reduce.5.cloned.1.call-update) | async-done | bytes 2097168 | tf_op jit(solution)/shard_map/psum | solution.py:60
  155.3 3.8 convert_add_fusion
  159.2 4.4 convolution_bitcast_fusion
  163.6 0.6 fusion.21
  164.2 0.7 and_reduce_fusion.3
  165.5 0.6 fusion.23
  166.7 0.6 multiply_rsqrt_fusion
  167.3 125.6 %all-reduce.7.cloned.1.call-done = f32[512,512]{0,1:T(8,128)} async-done(((f32[512,512]{0,1:T(8,128)}), f32[512,512]{0,1:T(8,128)}) %all-reduce.7.cloned.1.call-update) | async-done | bytes 1048592 | tf_op jit(solution)/shard_map/psum | solution.py:65
  292.9 5.5 fusion.1
  298.4 110.7 %all-reduce.1 = (f32[]{:T(128)}, f32[]{:T(128)}) all-reduce(f32[]{:T(128)} %get-tuple-element.53, f32[]{:T(128)} %get-tuple-element.52), channel_id=1, replica_groups=mesh['row'=16,'col'=32] {'row','col'}, use_global_device_ids=true, to_apply=%region_1.0 | all-reduce | flops 2 | bytes 16 | tf_op jit(solution)/shard_map/psum | solution.py:56
  410.4 4.5 multiply_reduce_fusion
  414.9 1.2 fusion.3
  416.5 24.4 %all-gather = f32[32768,1]{0,1:T(1,128)S(1)} all-gather(f32[1024,1]{0,1:T(1,128)S(1)} %slice.41), channel_id=2, replica_groups=mesh['row'=16,'col'=32] {'col'}, dimensions={0}, use_global_device_ids=true | all-gather | bytes 135168 | tf_op jit(solution)/shard_map/all_gather | solution.py:9
  441.5 0.9 reduce.11
  442.4 1.8 copy.22
  444.3 1.9 copy.16
  446.2 1.4 fusion.8
  447.9 19.9 %all-gather.1 = f32[16,1,512]{2,1,0:T(1,128)S(1)} all-gather(f32[1,1,512]{2,1,0:T(1,128)S(1)} %slice_bitcast_fusion), channel_id=1, replica_groups=mesh['row'=16,'col'=32] {'row'}, dimensions={0}, use_global_device_ids=true | all-gather | bytes 34816 | tf_op jit(solution)/shard_map/all_gather | solution.py:9
  469.9 6.1 %gather_fusion = f32[1024]{0:T(1024)S(1)} fusion(f32[524288]{0:T(1024)S(1)} %add.122, s32[1024]{0:T(1024)S(1)} %copy-done.4), kind=kCustom, calls=%fused_computation.clone | custom fusion | bytes 12288 | tf_op jit(solution)/shard_map/jit(_take)/gather | solution.py:101
  476.1 6.2 %gather_fusion.1 = f32[1024]{0:T(1024)S(1)} fusion(f32[524288]{0:T(1024)S(1)} %add.122, s32[1024]{0:T(1024)S(1)} %copy-done.7), kind=kCustom, calls=%fused_computation.1.clone | custom fusion | bytes 12288 | tf_op jit(solution)/shard_map/jit(_take)/gather | solution.py:101
  482.3 6.2 %gather_fusion.2 = f32[1024]{0:T(1024)S(1)} fusion(f32[524288]{0:T(1024)S(1)} %add.122, s32[1024]{0:T(1024)S(1)} %copy-done.5), kind=kCustom, calls=%fused_computation.2.clone | custom fusion | bytes 12288 | tf_op jit(solution)/shard_map/jit(_take)/gather | solution.py:101
  488.5 6.2 %gather_fusion.3 = f32[1024]{0:T(1024)S(1)} fusion(f32[524288]{0:T(1024)S(1)} %add.122, s32[1024]{0:T(1024)S(1)} %copy-done.6), kind=kCustom, calls=%fused_computation.3.clone | custom fusion | bytes 12288 | tf_op jit(solution)/shard_map/jit(_take)/gather | solution.py:101
  494.7 106.9 %all-reduce = (f32[]{:T(128)}, f32[1024]{0:T(1024)S(1)}) all-reduce(f32[]{:T(128)} %get-tuple-element.78, f32[1024]{0:T(1024)S(1)} %fusion.18), channel_id=1, replica_groups=mesh['row'=16,'col'=32] {'row','col'}, use_global_device_ids=true, to_apply=%region_7.0 | all-reduce | flops 1025 | bytes 8200 | tf_op jit(solution)/shard_map/psum | solution.py:76
  (54 shorter events, 5.2 us)
Async XLA Ops:
  7.2 152.0 %copy-start = (bf16[512,1024]{1,0:T(8,128)(2,1)S(1)}, bf16[512,1024]{1,0:T(8,128)(2,1)}, u32[]{:S(2)}) copy-start(bf16[512,1024]{1,0:T(8,128)(2,1)} %param.12) | copy-start | bytes 3145732
  7.2 3.6 copy-start.1
  7.2 3.6 copy-start.2
  7.2 148.1 %all-reduce.5.cloned.1.call-start = ((), (), s32[]{:S(2)}) async-start(), calls=%async_computation | async-start | bytes 4194304 | tf_op jit(solution)/shard_map/psum | solution.py:60
  10.8 282.2 %all-reduce.7.cloned.1.call-start = ((), (), s32[]{:S(2)}) async-start(), calls=%async_computation.1 | async-start | bytes 2097152 | tf_op jit(solution)/shard_map/psum | solution.py:65
  469.2 0.7 copy-start.4
  469.9 6.2 %copy-start.7 = (s32[1024]{0:T(1024)S(1)}, s32[1024]{0:T(1024)}, u32[]{:S(2)}) copy-start(s32[1024]{0:T(1024)} %fusion.22) | copy-start | bytes 12292
  476.1 6.2 %copy-start.5 = (s32[1024]{0:T(1024)S(1)}, s32[1024]{0:T(1024)}, u32[]{:S(2)}) copy-start(s32[1024]{0:T(1024)} %fusion.23) | copy-start | bytes 12292
  482.3 6.2 %copy-start.6 = (s32[1024]{0:T(1024)S(1)}, s32[1024]{0:T(1024)}, u32[]{:S(2)}) copy-start(s32[1024]{0:T(1024)} %fusion.24) | copy-start | bytes 12292
  488.4 6.2 %copy-start.8 = (pred[1024]{0:T(1024)(128)(4,1)S(1)}, pred[1024]{0:T(1024)(128)(4,1)}, u32[]{:S(2)}) copy-start(pred[1024]{0:T(1024)(128)(4,1)} %get-tuple-element.54) | copy-start | bytes 3076
  488.5 6.2 %copy-start.9 = (pred[1024]{0:T(1024)(128)(4,1)S(1)}, pred[1024]{0:T(1024)(128)(4,1)}, u32[]{:S(2)}) copy-start(pred[1024]{0:T(1024)(128)(4,1)} %get-tuple-element.55) | copy-start | bytes 3076
  488.5 6.2 %copy-start.10 = (pred[1024]{0:T(1024)(128)(4,1)S(1)}, pred[1024]{0:T(1024)(128)(4,1)}, u32[]{:S(2)}) copy-start(pred[1024]{0:T(1024)(128)(4,1)} %get-tuple-element.56) | copy-start | bytes 3076
  488.5 6.2 %copy-start.11 = (pred[1024]{0:T(1024)(128)(4,1)S(1)}, pred[1024]{0:T(1024)(128)(4,1)}, u32[]{:S(2)}) copy-start(pred[1024]{0:T(1024)(128)(4,1)} %get-tuple-element.57) | copy-start | bytes 3076
  488.5 114.4 %copy-start.3 = (f32[1024,1]{0,1:T(1,128)S(1)}, f32[1024,1]{0,1:T(1,128)}, u32[]{:S(2)}) copy-start(f32[1024,1]{0,1:T(1,128)} %multiply_rsqrt_fusion) | copy-start | bytes 12292
Sparse Core Ops, SparseCore 0:
  11.9 143.3 all-reduce.4
  163.7 129.1 all-reduce.6
where the time goes:
time: 612 us
  waiting for transfers between devices  270 us (44%)
  blocking collectives  262 us (43%)
  local copies, waits for them, and re-layouts  30.8 us (5%)
  matrix products  19.9 us (3%)
  between operations  18.2 us (3%)
  other arithmetic  10.5 us (2%)
    psum x1, waiting for transfers between devices, shards(): summed_right = lax.psum(partial_right, 'col')  144 us
    psum x1, waiting for transfers between devices, shards(): summed_left = lax.psum(partial_left, 'row')  126 us
    psum x1, blocking collectives, shards(): start_norm = lax.psum(jnp.sum(start_field * start_field), ('row', 'col'))  111 us
    psum x1, blocking collectives, shards(): fresh = lax.psum(jnp.sum(residual * residual), ('row', 'col'))  107 us
    all_gather x2, blocking collectives, prefix_2(): gathered = lax.all_gather(part, axis)  44.4 us
    gather x4, local copies, waits for them, and re-layouts, corner_value(): return jnp.where(inside, jnp.take(flat_prefix, position_flat), 0.0)  24.6 us
  transfers between devices with their start and end apart: 2, of which 2 were waited for; matrix products, arithmetic and copies ran while one was open for 1% of the time, Pallas kernels for 0%

commit v1 on v0

--- a/solution.py
+++ b/solution.py
@@ -57,7 +57,11 @@
     partial_right = lax.dot_general(
         right_side, theta_right, (((1,), (1,)), ((), ())), preferred_element_type=jnp.float32
     )
-    summed_right = lax.psum(partial_right, "col")
+    summed_right = partial_right
+    for hop_ in (1, 2, 4, 8, 16):
+        summed_right = summed_right + lax.ppermute(
+            summed_right, "col", [(dev, dev ^ hop_) for dev in range(32)]
+        )
     middle = start_field + jnp.dot(
         summed_right, right_wide, precision=highest, preferred_element_type=jnp.float32
     )

time: 612 us -> 678 us (1.11)
  waiting for transfers between devices: 270 us -> 320 us
  starting transfers between devices: 0.08 us -> 16.5 us
    ppermute x0 -> x5, waiting for transfers between devices: none -> 188 us  [shards(): lax.ppermute(summed_right, 'col', [(dev, dev ^ hop_) for dev in range(32)])]
    psum x1 -> x0, waiting for transfers between devices: 144 us -> none  [shards(): summed_right = lax.psum(partial_right, 'col')]
    ppermute x0 -> x5, starting transfers between devices: none -> 16.5 us  [shards(): lax.ppermute(summed_right, 'col', [(dev, dev ^ hop_) for dev in range(32)])]
  transfers between devices with their start and end apart: 2 -> 6, of which waited for: 2 -> 6; matrix products, arithmetic and copies ran while one was open for 1% -> 0% of each run, Pallas kernels for 0% -> 0%
where the time goes in v1:
time: 678 us
  waiting for transfers between devices  320 us (47%)
  blocking collectives  262 us (39%)
  local copies, waits for them, and re-layouts  31.3 us (5%)
  matrix products  20.8 us (3%)
  between operations  18.2 us (3%)
  starting transfers between devices  16.5 us (2%)
  other arithmetic  8.92 us (1%)
    ppermute x5, waiting for transfers between devices, shards(): lax.ppermute(summed_right, 'col', [(dev, dev ^ hop_) for dev in range(32)])  188 us
    psum x1, waiting for transfers between devices, shards(): summed_left = lax.psum(partial_left, 'row')  132 us
    psum x1, blocking collectives, shards(): start_norm = lax.psum(jnp.sum(start_field * start_field), ('row', 'col'))  111 us
    psum x1, blocking collectives, shards(): fresh = lax.psum(jnp.sum(residual * residual), ('row', 'col'))  107 us
    all_gather x2, blocking collectives, prefix_2(): gathered = lax.all_gather(part, axis)  44.1 us
    gather x4, local copies, waits for them, and re-layouts, corner_value(): return jnp.where(inside, jnp.take(flat_prefix, position_flat), 0.0)  24.6 us
    ppermute x5, starting transfers between devices, shards(): lax.ppermute(summed_right, 'col', [(dev, dev ^ hop_) for dev in range(32)])  16.5 us
  transfers between devices with their start and end apart: 6, of which 6 were waited for; matrix products, arithmetic and copies ran while one was open for 0% of the time, Pallas kernels for 0%

profile of v1, /device:TPU:1, one launch (start us, length us, event | category | flops | bytes accessed | tf_op | source)
XLA Modules:
  0.0 677.8 jit_solution(13868598141088137733)
XLA Ops:
  7.2 2.2 fusion.29
  9.4 8.8 %collective-permute-start = (f32[1024,512]{1,0:T(8,128)S(1)}, f32[1024,512]{1,0:T(8,128)S(1)}, u32[]{:S(2)}, u32[]{:S(2)}) collective-permute-start(f32[1024,512]{1,0:T(8,128)S(1)} %fusion.29), channel_id=1, source_target_pairs={{0,1},{1,0},{2,3},{3,2},{4,5},{5,4},{6,7},{7,6},{8,9},{9,8},{10,11... | collective-permute-start | bytes 6291464 | tf_op jit(solution)/shard_map/ppermute | solution.py:62
  18.2 3.8 collective-permute-done
  24.4 46.8 %collective-permute-done.1 = f32[1024,512]{1,0:T(8,128)S(1)} collective-permute-done((f32[1024,512]{1,0:T(8,128)S(1)}, f32[1024,512]{1,0:T(8,128)S(1)}, u32[]{:S(2)}, u32[]{:S(2)}) %collective-permute-start.1) | collective-permute-done | bytes 2097184 | tf_op jit(solution)/shard_map/ppermute | solution.py:62
  73.6 47.4 %collective-permute-done.2 = f32[1024,512]{1,0:T(8,128)S(1)} collective-permute-done((f32[1024,512]{1,0:T(8,128)S(1)}, f32[1024,512]{1,0:T(8,128)S(1)}, u32[]{:S(2)}, u32[]{:S(2)}) %collective-permute-start.2) | collective-permute-done | bytes 2097184 | tf_op jit(solution)/shard_map/ppermute | solution.py:62
  121.5 1.9 collective-permute-start.3
  123.4 45.0 %collective-permute-done.3 = f32[1024,512]{1,0:T(8,128)S(1)} collective-permute-done((f32[1024,512]{1,0:T(8,128)S(1)}, f32[1024,512]{1,0:T(8,128)S(1)}, u32[]{:S(2)}, u32[]{:S(2)}) %collective-permute-start.3) | collective-permute-done | bytes 2097184 | tf_op jit(solution)/shard_map/ppermute | solution.py:62
  168.9 1.9 collective-permute-start.4
  170.9 45.6 %collective-permute-done.4 = f32[1024,512]{1,0:T(8,128)} collective-permute-done((f32[1024,512]{1,0:T(8,128)S(1)}, f32[1024,512]{1,0:T(8,128)}, u32[]{:S(2)}, u32[]{:S(2)}) %collective-permute-start.4) | collective-permute-done | bytes 2097184 | tf_op jit(solution)/shard_map/ppermute | solution.py:62
  216.5 4.5 convert_add_fusion
  220.9 4.4 convolution_bitcast_fusion
  225.6 131.6 %all-reduce.4.cloned.1.call-done = f32[512,512]{0,1:T(8,128)} async-done(((f32[512,512]{0,1:T(8,128)}), f32[512,512]{0,1:T(8,128)}) %all-reduce.4.cloned.1.call-update) | async-done | bytes 1048592 | tf_op jit(solution)/shard_map/psum | solution.py:69
  357.2 5.5 fusion.1
  362.6 110.9 %all-reduce.1 = (f32[]{:T(128)}, f32[]{:T(128)}) all-reduce(f32[]{:T(128)} %get-tuple-element.53, f32[]{:T(128)} %get-tuple-element.52), channel_id=1, replica_groups=mesh['row'=16,'col'=32] {'row','col'}, use_global_device_ids=true, to_apply=%region_1.0 | all-reduce | flops 2 | bytes 16 | tf_op jit(solution)/shard_map/psum | solution.py:56
  474.9 4.5 multiply_reduce_fusion
  482.7 3.0 copy.16
  485.7 24.2 %all-gather = f32[32768,1]{0,1:T(1,128)S(1)} all-gather(f32[1024,1]{0,1:T(1,128)S(1)} %slice.41), channel_id=2, replica_groups=mesh['row'=16,'col'=32] {'col'}, dimensions={0}, use_global_device_ids=true | all-gather | bytes 135168 | tf_op jit(solution)/shard_map/all_gather | solution.py:9
  511.5 3.0 fusion.12
  514.8 19.9 %all-gather.1 = f32[16,1,512]{2,1,0:T(1,128)S(1)} all-gather(f32[1,1,512]{2,1,0:T(1,128)S(1)} %slice_bitcast_fusion), channel_id=1, replica_groups=mesh['row'=16,'col'=32] {'row'}, dimensions={0}, use_global_device_ids=true | all-gather | bytes 34816 | tf_op jit(solution)/shard_map/all_gather | solution.py:9
  536.3 6.2 gather_fusion
  542.5 6.2 gather_fusion.1
  548.6 6.2 gather_fusion.2
  554.8 6.2 gather_fusion.3
  561.0 106.9 %all-reduce = (f32[]{:T(128)}, f32[1024]{0:T(1024)S(1)}) all-reduce(f32[]{:T(128)} %get-tuple-element.78, f32[1024]{0:T(1024)S(1)} %fusion.22), channel_id=1, replica_groups=mesh['row'=16,'col'=32] {'row','col'}, use_global_device_ids=true, to_apply=%region_6.0 | all-reduce | flops 1025 | bytes 8200 | tf_op jit(solution)/shard_map/psum | solution.py:80
  (49 shorter events, 13.3 us)
Async XLA Ops:
  7.2 213.8 %copy-start = (bf16[512,1024]{1,0:T(8,128)(2,1)S(1)}, bf16[512,1024]{1,0:T(8,128)(2,1)}, u32[]{:S(2)}) copy-start(bf16[512,1024]{1,0:T(8,128)(2,1)} %param.12) | copy-start | bytes 3145732
  7.2 350.0 %all-reduce.4.cloned.1.call-start = ((), (), s32[]{:S(2)}) async-start(), calls=%async_computation | async-start | bytes 2097152 | tf_op jit(solution)/shard_map/psum | solution.py:69
  9.4 12.6 %collective-permute-start = (f32[1024,512]{1,0:T(8,128)S(1)}, f32[1024,512]{1,0:T(8,128)S(1)}, u32[]{:S(2)}, u32[]{:S(2)}) collective-permute-start(f32[1024,512]{1,0:T(8,128)S(1)} %fusion.29), channel_id=1, source_target_pairs={{0,1},{1,0},{2,3},{3,2},{4,5},{5,4},{6,7},{7,6},{8,9},{9,8},{10,11... | collective-permute-start | bytes 6291464 | tf_op jit(solution)/shard_map/ppermute | solution.py:62
  22.4 48.7 %collective-permute-start.1 = (f32[1024,512]{1,0:T(8,128)S(1)}, f32[1024,512]{1,0:T(8,128)S(1)}, u32[]{:S(2)}, u32[]{:S(2)}) collective-permute-start(f32[1024,512]{1,0:T(8,128)S(1)} %add.122), channel_id=1, source_target_pairs={{0,2},{1,3},{2,0},{3,1},{4,6},{5,7},{6,4},{7,5},{8,10},{9,11},{10,... | collective-permute-start | bytes 6291464 | tf_op jit(solution)/shard_map/ppermute | solution.py:62
  71.7 49.3 %collective-permute-start.2 = (f32[1024,512]{1,0:T(8,128)S(1)}, f32[1024,512]{1,0:T(8,128)S(1)}, u32[]{:S(2)}, u32[]{:S(2)}) collective-permute-start(f32[1024,512]{1,0:T(8,128)S(1)} %add.123), channel_id=1, source_target_pairs={{0,4},{1,5},{2,6},{3,7},{4,0},{5,1},{6,2},{7,3},{8,12},{9,13},{10,... | collective-permute-start | bytes 6291464 | tf_op jit(solution)/shard_map/ppermute | solution.py:62
  121.5 49.3 %copy-start.2 = (s32[1024,2]{0,1:T(2,128)S(1)}, s32[1024,2]{0,1:T(2,128)}, u32[]{:S(2)}) copy-start(s32[1024,2]{0,1:T(2,128)} %param.14) | copy-start | bytes 24580
  121.5 49.3 %copy-start.3 = (s32[1024,2]{0,1:T(2,128)S(1)}, s32[1024,2]{0,1:T(2,128)}, u32[]{:S(2)}) copy-start(s32[1024,2]{0,1:T(2,128)} %param.15) | copy-start | bytes 24580
  121.5 46.9 %collective-permute-start.3 = (f32[1024,512]{1,0:T(8,128)S(1)}, f32[1024,512]{1,0:T(8,128)S(1)}, u32[]{:S(2)}, u32[]{:S(2)}) collective-permute-start(f32[1024,512]{1,0:T(8,128)S(1)} %add.124), channel_id=1, source_target_pairs={{0,8},{1,9},{2,10},{3,11},{4,12},{5,13},{6,14},{7,15},{8,0},{9,1},... | collective-permute-start | bytes 6291464 | tf_op jit(solution)/shard_map/ppermute | solution.py:62
  168.9 2.0 copy-start.1
  168.9 47.6 %collective-permute-start.4 = (f32[1024,512]{1,0:T(8,128)S(1)}, f32[1024,512]{1,0:T(8,128)}, u32[]{:S(2)}, u32[]{:S(2)}) collective-permute-start(f32[1024,512]{1,0:T(8,128)S(1)} %add.125), channel_id=1, source_target_pairs={{0,16},{1,17},{2,18},{3,19},{4,20},{5,21},{6,22},{7,23},{8,24},{9,... | collective-permute-start | bytes 6291464 | tf_op jit(solution)/shard_map/ppermute | solution.py:62
Sparse Core Ops, SparseCore 0:
  225.5 131.5 all-reduce.3
